TPU v7x, 256 devices: a whole 4x4x8 slice. The times are simulated.
256 devices in a mesh: dp: 2 (over z_hi), tensor: 4 (over y), pool: 32 (over x, z_lo, core).
Axes of the slice: x: 4, y: 4, z: 8 (z_hi: 2, z_lo: 4; z = z_hi * 4 + z_lo), core: 2. Of those that a mesh axis runs over, the one named last changes fastest.
Arguments:
- tokens: bfloat16 [64, 1024, 4096], P(('dp', 'pool')), may hold values from -192 to 192, as said below
- w_hidden: bfloat16 [4096, 4096], P('pool', 'tensor'), may hold values from -0.09375 to 0.09375
- w_out: bfloat16 [4096, 256], P('tensor'), may hold values from -0.09375 to 0.09375
- bank: bfloat16 [32768, 256], P('pool'), may hold values from -0.5 to 0.5
- item_ids: int32 [32768], P('pool'), may hold values from 0 to 1048575
- log_freq: bfloat16 [1048576], replicated, may hold values from -14 to -6
- positives: int32 [64, 1024], P(('dp', 'pool'), 'tensor'), may hold values from 0 to 32767
- new_items: bfloat16 [8192, 256], P('pool'), may hold values from -0.5 to 0.5
- new_owner: int32 [8192, 1], P('pool'), may hold values from 0 to 31; in each aligned block of 256 rows (0 to 255, 256 to 511, ...) at most 16 rows name the same one
- queue_head: int32 [32], P('pool'), may hold values from 0 to 1023
Outputs:
- query_loss: float32 [64, 1024], P(('dp', 'pool'), 'tensor')
- new_bank: bfloat16 [32768, 256], P('pool')
Inputs may be any that keep to these rules, and one draw needn't show every extreme that they name: `tokens`: float values within the range. `new_owner`: among the 256 new rows of one pool index, no shard is named by more than 16 rows, a bound that some block reaches.
All inputs are finite; a program needn't handle non-finite values.
Results may differ from a plain program's by a relative error of at most 0.002.
Values may be sent and summed in bfloat16 or wider, within the bound.
A program may use at most 128 MiB of HBM per device.

v0:
```python
import jax
import jax.numpy as jnp
from jax import lax
from jax.sharding import Mesh
from jax.sharding import PartitionSpec as P

POOL = ("pool_0", "pool_1", "pool_2")
DP_POOL = ("dp", "pool_0", "pool_1", "pool_2")
inv_temp = 5.0


def split_up(x, dim, count):
    before, after = (x.shape[:dim], x.shape[dim + 1 :])
    return jnp.moveaxis(x.reshape(*before, count, -1, *after), dim, 0)


def sum_at_owner(x, axis, dim):
    count = lax.axis_size(axis)
    blocks = lax.all_to_all(split_up(x, dim, count), axis, 0, 0, tiled=True)
    return jnp.sum(blocks, axis=0)


def all_in_one(x, axis):
    leaves = jax.tree.leaves(x)
    turns = sorted(range(len(leaves)), key=lambda k: -leaves[k].size)
    width = (1, *leaves[turns[0]].shape)[-1]
    lines = [
        jnp.pad(leaves[k].reshape(-1), (0, -leaves[k].size % width)).reshape(-1, width)
        for k in turns
    ]
    both, at, found = (lax.all_gather(jnp.concatenate(lines), axis), 0, {})
    for k, line in zip(turns, lines):
        section = both[:, at : at + len(line)].reshape(len(both), -1)
        found[k] = section[:, : leaves[k].size].reshape(-1, *leaves[k].shape)
        at += len(line)
    numbers = iter(range(len(leaves)))
    return jax.tree.map(lambda _: found[next(numbers)], x)


def joined_all(x, axes, combine):
    for axis in axes:
        pieces = all_in_one(x, axis)
        x = jax.tree.map(lambda part: part[0], pieces)
        for k in range(1, lax.axis_size(axis)):
            x = combine(x, jax.tree.map(lambda part: part[k], pieces))
    return x


def copy_for_each(x, axis):
    copies = jnp.broadcast_to(x, (lax.axis_size(axis), *x.shape))
    return lax.all_to_all(copies, axis, split_axis=0, concat_axis=0, tiled=True)


def folded_in_pairs(pieces, combine):
    while len(jax.tree.leaves(pieces)[0]) > 1:
        pieces = jax.vmap(combine)(*(pieces[side::2] for side in (0, 1)))
    return pieces[0]


def entering(x, axis, combine, identity):
    count, position = (lax.axis_size(axis), lax.axis_index(axis))
    passed = jnp.arange(count) < position

    def kept(part, zero, own):
        part = jnp.where(
            passed.reshape(-1, *(1 for _ in own.shape)), part, jnp.asarray(zero, own.dtype)
        )
        return part

    pieces = copy_for_each(x, axis)
    return folded_in_pairs(kept(pieces, identity, x), combine)


def local_stats(query_rows, target_rows, bank, offsets, base_column):
    row_count = query_rows.shape[0]
    bank_rows = bank.shape[0]
    block_width = 512
    block_count = bank_rows // block_width
    blocks = bank.reshape(block_count, block_width, bank.shape[1])
    shifts = offsets.reshape(block_count, block_width)

    def block_step(running, inputs):
        run_max, run_sum, run_pos = running
        bank_block, block_offsets, block_index = inputs
        logits = (
            inv_temp * jnp.dot(query_rows, bank_block.T, preferred_element_type=jnp.float32)
            - block_offsets[None, :]
        )
        next_max = jnp.maximum(run_max, jnp.max(logits, axis=1))
        run_sum = run_sum * jnp.exp(run_max - next_max) + jnp.sum(
            jnp.exp(logits - next_max[:, None]), axis=1
        )
        columns = base_column + block_index * block_width + jnp.arange(block_width, dtype=jnp.int32)
        run_pos = run_pos + jnp.sum(
            jnp.where(columns[None, :] == target_rows[:, None], logits, 0.0), axis=1
        )
        return ((next_max, run_sum, run_pos), None)

    initial = (
        jnp.full((row_count,), -jnp.inf, jnp.float32),
        jnp.zeros((row_count,), jnp.float32),
        jnp.zeros((row_count,), jnp.float32),
    )
    final, _ = lax.scan(
        block_step, initial, (blocks, shifts, jnp.arange(block_count, dtype=jnp.int32))
    )
    return final


def combine(earlier_part, later_part):
    both_max = jnp.maximum(earlier_part[0], later_part[0])
    both_sum = earlier_part[1] * jnp.exp(earlier_part[0] - both_max) + later_part[1] * jnp.exp(
        later_part[0] - both_max
    )
    return (both_max, both_sum, earlier_part[2] + later_part[2])


def add_counts(earlier_part, later_part):
    return earlier_part + later_part


def body(
    tokens, w_hidden, w_out, bank, item_ids, log_freq, positives, new_items, new_owner, queue_head
):
    token_rows = tokens[0]
    pre_act = jnp.dot(
        token_rows,
        lax.all_gather(w_hidden, POOL, axis=0, tiled=True),
        preferred_element_type=jnp.float32,
    )
    hidden = jnp.maximum(pre_act, 0.0).astype(jnp.bfloat16)
    partial_value = jnp.dot(hidden, w_out, preferred_element_type=jnp.float32)
    queries = sum_at_owner(partial_value, "tensor", 0).astype(jnp.bfloat16)
    offsets = jnp.take(log_freq, item_ids).astype(jnp.float32)
    own_index = lax.axis_index(POOL)
    base_column = own_index * bank.shape[0]
    query_piece = lax.all_gather(queries[None], POOL, axis=0, tiled=True)
    target_piece = lax.all_gather(positives, POOL, axis=0, tiled=True)
    groups_in = query_piece.shape[0]
    run_max, run_sum, run_pos = local_stats(
        query_piece.reshape(-1, query_piece.shape[2]),
        target_piece.reshape(-1),
        bank,
        offsets,
        base_column,
    )
    maxima = run_max.reshape(groups_in, -1)
    totals = run_sum.reshape(groups_in, -1)
    scores = run_pos.reshape(groups_in, -1)
    maxima, totals, scores = (maxima, totals, scores)
    maxima, totals, scores = joined_all((maxima, totals, scores), POOL, combine)
    own_max = lax.dynamic_slice_in_dim(maxima, own_index, 1, 0)
    own_sum = lax.dynamic_slice_in_dim(totals, own_index, 1, 0)
    own_pos = lax.dynamic_slice_in_dim(scores, own_index, 1, 0)
    query_loss = own_max + jnp.log(own_sum) - own_pos
    owners = new_owner[:, 0]
    head_slot = queue_head[0]
    shard_rows = bank.shape[0]
    peer_count = lax.axis_size(POOL)
    local_rows = new_items.shape[0]
    capacity = 2 * local_rows // peer_count
    onehot = (owners[:, None] == jnp.arange(peer_count, dtype=jnp.int32)[None, :]).astype(jnp.int32)
    counts = jnp.sum(onehot, axis=0, dtype=jnp.int32)
    before = jnp.sum(
        (jnp.cumsum(onehot, axis=0, dtype=jnp.int32) - onehot) * onehot, axis=1, dtype=jnp.int32
    )
    earlier = entering(counts, POOL, add_counts, jnp.zeros_like(counts))
    ranks = before + jnp.sum(onehot * earlier[None, :], axis=1, dtype=jnp.int32)
    send_pos = owners * capacity + before
    rows_out = (
        jnp.zeros((peer_count * capacity, new_items.shape[1]), jnp.bfloat16)
        .at[send_pos]
        .set(new_items)
    )
    ranks_out = jnp.full((peer_count * capacity,), -1, jnp.int32).at[send_pos].set(ranks)
    rows_in, ranks_in = (
        lax.all_to_all(
            rows_out.reshape(peer_count, capacity, -1),
            POOL,
            split_axis=0,
            concat_axis=0,
            tiled=True,
        ),
        lax.all_to_all(
            ranks_out.reshape(peer_count, capacity), POOL, split_axis=0, concat_axis=0, tiled=True
        ),
    )
    local_slots = jnp.where(ranks_in >= 0, (head_slot + ranks_in) % shard_rows, shard_rows).reshape(
        -1
    )
    new_bank = bank.at[local_slots].set(rows_in.reshape(-1, new_items.shape[1]), mode="drop")
    return (query_loss, new_bank)


def solution(mesh):
    finer = Mesh(
        mesh.devices.reshape(mesh.shape["dp"], mesh.shape["tensor"], 4, 4, 2),
        ("dp", "tensor", "pool_0", "pool_1", "pool_2"),
    )
    in_specs = (
        P(DP_POOL, None, None),
        P(POOL, "tensor"),
        P("tensor", None),
        P(POOL, None),
        P(POOL),
        P(),
        P(DP_POOL, "tensor"),
        P(POOL, None),
        P(POOL, None),
        P(POOL),
    )
    out_specs = (P(DP_POOL, "tensor"), P(POOL, None))
    return jax.shard_map(body, mesh=finer, in_specs=in_specs, out_specs=out_specs, check_vma=False)
```

profile of v0, /device:TPU:1, one launch (start us, length us, event | category | flops | bytes accessed | tf_op | source)
XLA Modules:
  0.0 274.3 jit_solution(2599973721477552642)
XLA Ops:
  7.2 0.7 all-gather.8.cloned.1.call-update
  8.0 74.6 %all-gather.8.cloned.1.call-done = bf16[4096,1024]{1,0:T(8,128)(2,1)} async-done(((bf16[128,1024]{1,0:T(8,128)(2,1)}), bf16[4096,1024]{1,0:T(8,128)(2,1)}) %all-gather.8.cloned.1.call-update) | async-done | bytes 8388624 | tf_op jit(solution)/shard_map/all_gather | solution.py:128
  82.6 16.4 %fusion.12 = f32[1024,256]{1,0:T(8,128)} fusion(bf16[1024,256]{1,0:T(8,128)(2,1)} %param.14, bf16[4096,1024]{1,0:T(8,128)(2,1)} %all-gather.8.cloned.1.call-done, bf16[1,1024,4096]{2,1,0:T(8,128)(2,1)} %param.12), kind=kOutput, calls=%fused_computation.22 | convolution fusion | flops 9128902656 | bytes 18350080 | tf_op jit(solution)/shard_map/dot_general | solution.py:132
  98.9 19.1 %all_to_all.28 = f32[4,256,256]{2,1,0:T(8,128)} all-to-all(f32[4,256,256]{2,1,0:T(8,128)} %bitcast.252), channel_id=1, replica_groups=mesh['dp'=2,'tensor'=4,'pool_0'=4,'pool_1'=4,'pool_2'=2] {'tensor'}, dimensions={0} | all-to-all | bytes 2097152 | tf_op jit(solution)/shard_map/all_to_all | solution.py:19
  118.0 2.0 reduce_sum.56
  120.0 0.1 convert_reduce_fusion
  120.2 0.6 broadcast_in_dim.52
  120.8 6.5 %all-to-all-start.1 = ((s32[32,1,32]{2,1,0:T(1,128)}), s32[32,1,32]{2,1,0:T(1,128)S(1)}, u32[]{:S(2)}, u32[]{:S(2)}) async-start(s32[32,1,32]{2,1,0:T(1,128)} %broadcast_in_dim.52), calls=%async_computation.1 | async-start | bytes 32768 | tf_op jit(solution)/shard_map/all_to_all | solution.py:51
  127.3 6.8 %gather_fusion = bf16[1024]{0:T(1024)(128)(2,1)S(1)} fusion(bf16[1048576]{0:T(1024)(128)(2,1)S(1)} %copy-done, s32[1024]{0:T(1024)S(1)} %fusion.46), kind=kCustom, calls=%fused_computation | custom fusion | bytes 8192 | tf_op jit(solution)/shard_map/jit(_take)/gather | solution.py:134
  134.1 0.6 reduce-window.6
  134.7 0.2 slice_reduce_fusion
  135.3 0.1 select_reduce_fusion
  135.4 1.4 scatter_custom_fusion
  136.8 0.7 all_to_all.21
  137.5 7.7 %all-to-all-start.2 = ((s32[32,1,16]{2,1,0:T(1,128)}), s32[32,1,16]{2,1,0:T(1,128)S(1)}, u32[]{:S(2)}, u32[]{:S(2)}) async-start(s32[32,1,16]{2,1,0:T(1,128)} %bitcast.37), calls=%async_computation.2 | async-start | bytes 32768 | tf_op jit(solution)/shard_map/all_to_all | solution.py:184
  145.2 43.7 %all-gather.4 = s32[32,1,256]{2,1,0:T(1,128)S(1)} all-gather(s32[1,1,256]{2,1,0:T(1,128)S(1)} %bitcast.259), channel_id=1, replica_groups=mesh['dp'=2,'tensor'=4,'pool_0'=4,'pool_1'=4,'pool_2'=2] {'pool_0','pool..., dimensions={0}, use_global_device_ids=true | all-gather | bytes 33792 | tf_op jit(solution)/shard_map/all_gather | solution.py:138
  189.6 2.5 scatter_custom_fusion.1
  192.1 3.7 %all-to-all-start.3 = ((bf16[32,16,256]{2,1,0:T(8,128)(2,1)}), bf16[32,16,256]{2,1,0:T(8,128)(2,1)S(1)}, u32[]{:S(2)}, u32[]{:S(2)}) async-start(bf16[32,16,256]{2,1,0:T(8,128)(2,1)} %bitcast.40), calls=%async_computation.3 | async-start | bytes 524288 | tf_op jit(solution)/shard_map/all_to_all | solution.py:177
  195.8 0.1 ge.29
  196.1 37.4 %while.15 = (s32[]{:T(128)}, f32[8192]{0:T(1024)S(1)}, f32[8192]{0:T(1024)S(1)}, f32[8192]{0:T(1024)S(1)}, bf16[2,512,256]{2,1,0:T(8,128)(2,1)S(1)}, /*index=5*/...) while((s32[]{:T(128)}, f32[8192]{0:T(1024)S(1)}, ...), condition=%wide.region_5.6_spmd.clone, body=%wide.region_1.5_spmd.clone.sunk | while | flops 2181087744 | bytes 38676668 | solution.py:104
  196.2 9.2 %fusion.74 = (f32[8192]{0:T(1024)S(1)}, f32[512,8192]{1,0:T(8,128)}) fusion(f32[512]{0:T(512)S(1)} %bitcast.241, bf16[8192,256]{1,0:T(8,128)(2,1)} %get-tuple-element.234, bf16[2,512,256]{2,1,0:T(8,128)(2,1)S(1)} %get-tuple-element.233, s32[]{:T(128)S(6)} %copy.27), kind=kOutput, calls=%fused_computation.130.clone.1 | convolution fusion | flops 2160058368 | bytes 21268484 | tf_op jit(solution)/shard_map/while/body/eval_jaxpr/dot_general | solution.py:86
  205.4 0.6 dynamic_slice.94
  206.7 8.1 %fusion.75 = (f32[8192]{0:T(1024)S(1)}, f32[8192]{0:T(1024)S(1)}) fusion(f32[512,8192]{1,0:T(8,128)} %get-tuple-element.198, s32[8192]{0:T(1024)S(1)} %bitcast.242, s32[512]{0:T(512)S(1)} %iota_add_fusion.2, f32[8192]{0:T(1024)S(1)} %select_maximum_fusion.2), kind=kLoop, calls=%fused_computation.8.clone.1 | loop fusion | flops 20955136 | bytes 16910336 | tf_op jit(solution)/shard_map/while/body/eval_jaxpr/reduce_sum | solution.py:94
  214.8 9.2 %fusion.74 = (f32[8192]{0:T(1024)S(1)}, f32[512,8192]{1,0:T(8,128)}) fusion(f32[512]{0:T(512)S(1)} %bitcast.241, bf16[8192,256]{1,0:T(8,128)(2,1)} %get-tuple-element.234, bf16[2,512,256]{2,1,0:T(8,128)(2,1)S(1)} %get-tuple-element.233, s32[]{:T(128)S(6)} %copy.27), kind=kOutput, calls=%fused_computation.130.clone.1 | convolution fusion | flops 2160058368 | bytes 21268484 | tf_op jit(solution)/shard_map/while/body/eval_jaxpr/dot_general | solution.py:86
  224.1 0.6 dynamic_slice.94
  225.3 8.1 %fusion.75 = (f32[8192]{0:T(1024)S(1)}, f32[8192]{0:T(1024)S(1)}) fusion(f32[512,8192]{1,0:T(8,128)} %get-tuple-element.198, s32[8192]{0:T(1024)S(1)} %bitcast.242, s32[512]{0:T(512)S(1)} %iota_add_fusion.2, f32[8192]{0:T(1024)S(1)} %select_maximum_fusion.2), kind=kLoop, calls=%fused_computation.8.clone.1 | loop fusion | flops 20955136 | bytes 16910336 | tf_op jit(solution)/shard_map/while/body/eval_jaxpr/reduce_sum | solution.py:94
  233.6 10.9 %all-gather.1 = f32[384,256]{1,0:T(8,128)S(1)} all-gather(f32[96,256]{1,0:T(8,128)S(1)} %pad_maximum_fusion), channel_id=3, replica_groups=mesh['dp'=2,'tensor'=4,'pool_0'=4,'pool_1'=4,'pool_2'=2] {'pool_0'}, dimensions={0}, use_global_device_ids=true | all-gather | bytes 491520 | tf_op jit(solution)/shard_map/all_gather | solution.py:31
  244.6 11.7 %all-gather.2 = f32[384,256]{1,0:T(8,128)S(1)} all-gather(f32[96,256]{1,0:T(8,128)S(1)} %pad_maximum_fusion.1), channel_id=4, replica_groups=mesh['dp'=2,'tensor'=4,'pool_0'=4,'pool_1'=4,'pool_2'=2] {'pool_1'}, dimensions={0}, use_global_device_ids=true | all-gather | bytes 491520 | tf_op jit(solution)/shard_map/all_gather | solution.py:31
  256.3 7.7 %all-gather.3 = f32[192,256]{1,0:T(8,128)S(1)} all-gather(f32[96,256]{1,0:T(8,128)S(1)} %pad_maximum_fusion.2), channel_id=5, replica_groups=mesh['dp'=2,'tensor'=4,'pool_0'=4,'pool_1'=4,'pool_2'=2] {'pool_2'}, dimensions={0}, use_global_device_ids=true | all-gather | bytes 294912 | tf_op jit(solution)/shard_map/all_gather | solution.py:31
  264.1 2.6 scatter_fusion
  266.7 0.7 fusion.54
  267.4 0.1 copy-done.1
  (74 shorter events, 1.0 us)
Async XLA Ops:
  7.2 120.1 %copy-start = (bf16[1048576]{0:T(1024)(128)(2,1)S(1)}, bf16[1048576]{0:T(1024)(128)(2,1)}, u32[]{:S(2)}) copy-start(bf16[1048576]{0:T(1024)(128)(2,1)} %param.17) | copy-start | bytes 6291460
  7.2 75.4 %all-gather.8.cloned.1.call-start = ((), (), s32[]{:S(2)}) async-start(), calls=%async_computation.4 | async-start | bytes 8650752 | tf_op jit(solution)/shard_map/all_gather | solution.py:128
  7.9 112.1 %copy-start.4 = (s32[256,1]{0,1:T(1,128)S(1)}, s32[256,1]{0,1:T(1,128)}, u32[]{:S(2)}) copy-start(s32[256,1]{0,1:T(1,128)} %param.20) | copy-start | bytes 3076
  7.9 119.3 %copy-start.3 = (s32[1024]{0:T(1024)S(1)}, s32[1024]{0:T(1024)}, u32[]{:S(2)}) copy-start(s32[1024]{0:T(1024)} %param.16) | copy-start | bytes 12292
  7.9 137.2 %copy-start.5 = (s32[1,256]{1,0:T(1,128)S(1)}, s32[1,256]{1,0:T(1,128)}, u32[]{:S(2)}) copy-start(s32[1,256]{1,0:T(1,128)} %param.18) | copy-start | bytes 3076
  7.9 188.2 %copy-start.2 = (bf16[1024,256]{1,0:T(8,128)(2,1)S(1)}, bf16[1024,256]{1,0:T(8,128)(2,1)}, u32[]{:S(2)}) copy-start(bf16[1024,256]{1,0:T(8,128)(2,1)} %param.15) | copy-start | bytes 1572868
  8.0 188.2 %all-gather.10.cloned.1.call-start = ((), (), s32[]{:S(2)}) async-start(), calls=%async_computation.5 | async-start | bytes 4325376 | tf_op jit(solution)/shard_map/all_gather | solution.py:137
  120.8 14.2 %all-to-all-start.1 = ((s32[32,1,32]{2,1,0:T(1,128)}), s32[32,1,32]{2,1,0:T(1,128)S(1)}, u32[]{:S(2)}, u32[]{:S(2)}) async-start(s32[32,1,32]{2,1,0:T(1,128)} %broadcast_in_dim.52), calls=%async_computation.1 | async-start | bytes 32768 | tf_op jit(solution)/shard_map/all_to_all | solution.py:51
  137.5 54.6 %all-to-all-start.2 = ((s32[32,1,16]{2,1,0:T(1,128)}), s32[32,1,16]{2,1,0:T(1,128)S(1)}, u32[]{:S(2)}, u32[]{:S(2)}) async-start(s32[32,1,16]{2,1,0:T(1,128)} %bitcast.37), calls=%async_computation.2 | async-start | bytes 32768 | tf_op jit(solution)/shard_map/all_to_all | solution.py:184
  192.1 72.0 %all-to-all-start.3 = ((bf16[32,16,256]{2,1,0:T(8,128)(2,1)}), bf16[32,16,256]{2,1,0:T(8,128)(2,1)S(1)}, u32[]{:S(2)}, u32[]{:S(2)}) async-start(bf16[32,16,256]{2,1,0:T(8,128)(2,1)} %bitcast.40), calls=%async_computation.3 | async-start | bytes 524288 | tf_op jit(solution)/shard_map/all_to_all | solution.py:177
  266.7 0.8 copy-start.1
Sparse Core Ops, SparseCore 0:
  9.8 72.6 all-gather.7
  120.2 60.7 all-gather.9
where the time goes:
time: 275 us; the launch traced here: 274 us
  blocking collectives  93.1 us (34%)
  waiting for transfers between devices  75.3 us (27%)
  matrix products  34.8 us (13%)
  other arithmetic  20.1 us (7%)
  starting transfers between devices  17.9 us (7%)
  local copies, waits for them, and re-layouts  16.6 us (6%)
  between operations  15 us (5%)
    all_gather x1, waiting for transfers between devices, body(): lax.all_gather(w_hidden, POOL, axis=0, tiled=True)  74.6 us
    all_gather x1, blocking collectives, body(): target_piece = lax.all_gather(positives, POOL, axis=0, tiled=True)  43.7 us
    all_gather x3, blocking collectives, all_in_one(): both, at, found = (lax.all_gather(jnp.concatenate(lines), axis), 0, {})  30.3 us
    all_to_all x1, blocking collectives, sum_at_owner(): blocks = lax.all_to_all(split_up(x, dim, count), axis, 0, 0, tiled=True)  19.1 us
    dot_general x2, matrix products, block_step(): jnp.dot(query_rows, bank_block.T, preferred_element_type=jnp.float32)  18.5 us
    dot_general x1, matrix products, body(): partial_value = jnp.dot(hidden, w_out, preferred_element_type=jnp.float32)  16.4 us
    reduce_sum x2, other arithmetic, block_step(): jnp.sum(jnp.where(columns[None, :] == target_rows[:, None], logits, 0.0),...  16.2 us
    all_to_all x1, starting transfers between devices, body(): lax.all_to_all(ranks_out.reshape(peer_count, capacity), POOL, split_axis=...  7.69 us
  transfers between devices with their start and end apart: 5, of which 1 were waited for; matrix products, arithmetic and copies ran while one was open for 18% of the time, Pallas kernels for 0%

commit v1 on v0

--- a/solution.py
+++ b/solution.py
@@ -123,10 +123,18 @@
     tokens, w_hidden, w_out, bank, item_ids, log_freq, positives, new_items, new_owner, queue_head
 ):
     token_rows = tokens[0]
+
+    def chains_see(shard_axis, original):
+        windows = []
+        for _ in range(lax.axis_size(shard_axis)):
+            windows.append(original)
+        inter = jnp.stack(windows, axis=0)
+        block_now = lax.all_to_all(inter, shard_axis, 0, 0)
+        reply = jnp.concatenate(block_now, 0)
+        return reply
+
     pre_act = jnp.dot(
-        token_rows,
-        lax.all_gather(w_hidden, POOL, axis=0, tiled=True),
-        preferred_element_type=jnp.float32,
+        token_rows, chains_see(POOL, original=w_hidden), preferred_element_type=jnp.float32
     )
     hidden = jnp.maximum(pre_act, 0.0).astype(jnp.bfloat16)
     partial_value = jnp.dot(hidden, w_out, preferred_element_type=jnp.float32)

time: 275 us -> 395 us (1.44)
  blocking collectives: 93.1 us -> 288 us
  waiting for transfers between devices: 75.3 us -> 0.04 us
    all_to_all x0 -> x1, blocking collectives: none -> 195 us  [chains_see(): block_now = lax.all_to_all(inter, shard_axis, 0, 0)]
    all_gather x1 -> x0, waiting for transfers between devices: 74.6 us -> none  [body(): lax.all_gather(w_hidden, POOL, axis=0, tiled=True)]
  transfers between devices with their start and end apart: 5 -> 4, of which waited for: 1 -> 0; matrix products, arithmetic and copies ran while one was open for 18% -> 12% of each run, Pallas kernels for 0% -> 0%
where the time goes in v1:
time: 395 us
  blocking collectives  288 us (73%)
  matrix products  34.8 us (9%)
  other arithmetic  20.1 us (5%)
  local copies, waits for them, and re-layouts  18.8 us (5%)
  starting transfers between devices  16.4 us (4%)
  between operations  15 us (4%)
    all_to_all x1, blocking collectives, chains_see(): block_now = lax.all_to_all(inter, shard_axis, 0, 0)  195 us
    all_gather x1, blocking collectives, body(): target_piece = lax.all_gather(positives, POOL, axis=0, tiled=True)  43.7 us
    all_gather x3, blocking collectives, all_in_one(): both, at, found = (lax.all_gather(jnp.concatenate(lines), axis), 0, {})  30.3 us
    all_to_all x1, blocking collectives, sum_at_owner(): blocks = lax.all_to_all(split_up(x, dim, count), axis, 0, 0, tiled=True)  19 us
    dot_general x2, matrix products, block_step(): jnp.dot(query_rows, bank_block.T, preferred_element_type=jnp.float32)  18.5 us
    dot_general x1, matrix products, body(): partial_value = jnp.dot(hidden, w_out, preferred_element_type=jnp.float32)  16.4 us
    reduce_sum x2, other arithmetic, block_step(): jnp.sum(jnp.where(columns[None, :] == target_rows[:, None], logits, 0.0),...  16.2 us
  transfers between devices with their start and end apart: 4, of which 0 were waited for; matrix products, arithmetic and copies ran while one was open for 12% of the time, Pallas kernels for 0%

profile of v1, /device:TPU:1, one launch (start us, length us, event | category | flops | bytes accessed | tf_op | source)
XLA Modules:
  0.0 394.7 jit_solution(17531096805542949611)
XLA Ops:
  7.2 2.2 stack.2
  9.4 195.2 %all_to_all.33 = bf16[32,128,1024]{2,1,0:T(8,128)(2,1)} all-to-all(bf16[32,128,1024]{2,1,0:T(8,128)(2,1)S(1)} %stack.2), channel_id=1, replica_groups=mesh['dp'=2,'tensor'=4,'pool_0'=4,'pool_1'=4,'pool_2'=2] {'pool_0','pool..., dimensions={0} | all-to-all | bytes 16777216 | tf_op jit(solution)/shard_map/all_to_all | solution.py:132
  204.6 16.4 %fusion.12 = f32[1024,256]{1,0:T(8,128)} fusion(bf16[1024,256]{1,0:T(8,128)(2,1)S(1)} %copy-done.6, bf16[4096,1024]{1,0:T(8,128)(2,1)} %bitcast.242, bf16[1,1024,4096]{2,1,0:T(8,128)(2,1)} %param.12), kind=kOutput, calls=%fused_computation.22 | convolution fusion | flops 9128902656 | bytes 18350080 | tf_op jit(solution)/shard_map/dot_general | solution.py:140
  221.0 19.0 %all_to_all.34 = f32[4,256,256]{2,1,0:T(8,128)} all-to-all(f32[4,256,256]{2,1,0:T(8,128)} %bitcast.254), channel_id=1, replica_groups=mesh['dp'=2,'tensor'=4,'pool_0'=4,'pool_1'=4,'pool_2'=2] {'tensor'}, dimensions={0} | all-to-all | bytes 2097152 | tf_op jit(solution)/shard_map/all_to_all | solution.py:19
  240.0 2.0 reduce_sum.56
  242.0 0.1 convert_reduce_fusion
  242.1 0.6 broadcast_in_dim.52
  242.7 4.8 %all-to-all-start.2 = ((s32[32,1,32]{2,1,0:T(1,128)}), s32[32,1,32]{2,1,0:T(1,128)S(1)}, u32[]{:S(2)}, u32[]{:S(2)}) async-start(s32[32,1,32]{2,1,0:T(1,128)} %broadcast_in_dim.52), calls=%async_computation.2 | async-start | bytes 32768 | tf_op jit(solution)/shard_map/all_to_all | solution.py:51
  247.6 6.8 %gather_fusion = bf16[1024]{0:T(1024)(128)(2,1)S(1)} fusion(bf16[1048576]{0:T(1024)(128)(2,1)S(1)} %copy-done, s32[1024]{0:T(1024)S(1)} %fusion.46), kind=kCustom, calls=%fused_computation | custom fusion | bytes 8192 | tf_op jit(solution)/shard_map/jit(_take)/gather | solution.py:142
  254.4 0.6 reduce-window.6
  255.0 0.2 slice_reduce_fusion
  255.6 0.1 select_reduce_fusion
  255.7 1.4 scatter_custom_fusion
  257.1 0.7 all_to_all.25
  257.8 7.8 %all-to-all-start.3 = ((s32[32,1,16]{2,1,0:T(1,128)}), s32[32,1,16]{2,1,0:T(1,128)S(1)}, u32[]{:S(2)}, u32[]{:S(2)}) async-start(s32[32,1,16]{2,1,0:T(1,128)} %bitcast.38), calls=%async_computation.3 | async-start | bytes 32768 | tf_op jit(solution)/shard_map/all_to_all | solution.py:192
  265.6 43.7 %all-gather.4 = s32[32,1,256]{2,1,0:T(1,128)S(1)} all-gather(s32[1,1,256]{2,1,0:T(1,128)S(1)} %bitcast.261), channel_id=1, replica_groups=mesh['dp'=2,'tensor'=4,'pool_0'=4,'pool_1'=4,'pool_2'=2] {'pool_0','pool..., dimensions={0}, use_global_device_ids=true | all-gather | bytes 33792 | tf_op jit(solution)/shard_map/all_gather | solution.py:146
  309.9 2.5 scatter_custom_fusion.1
  312.5 3.7 all-to-all-start.4
  316.4 0.1 ge.29
  316.5 37.3 %while.15 = (s32[]{:T(128)}, f32[8192]{0:T(1024)S(1)}, f32[8192]{0:T(1024)S(1)}, f32[8192]{0:T(1024)S(1)}, bf16[2,512,256]{2,1,0:T(8,128)(2,1)S(1)}, /*index=5*/...) while((s32[]{:T(128)}, f32[8192]{0:T(1024)S(1)}, ...), condition=%wide.region_5.6_spmd.clone, body=%wide.region_1.5_spmd.clone.sunk | while | flops 2181087744 | bytes 38676660 | solution.py:104
  316.6 9.2 %fusion.74 = (f32[8192]{0:T(1024)S(1)}, f32[512,8192]{1,0:T(8,128)}) fusion(f32[512]{0:T(512)S(1)} %bitcast.243, bf16[8192,256]{1,0:T(8,128)(2,1)} %get-tuple-element.234, bf16[2,512,256]{2,1,0:T(8,128)(2,1)S(1)} %get-tuple-element.233, s32[]{:T(128)} %get-tuple-element.216), kind=kOutput, calls=%fused_computation.130.clone.1 | convolution fusion | flops 2160058368 | bytes 21268484 | tf_op jit(solution)/shard_map/while/body/eval_jaxpr/dot_general | solution.py:86
  325.8 0.6 dynamic_slice.94
  327.0 8.1 %fusion.75 = (f32[8192]{0:T(1024)S(1)}, f32[8192]{0:T(1024)S(1)}) fusion(f32[512,8192]{1,0:T(8,128)} %get-tuple-element.198, s32[8192]{0:T(1024)S(1)} %bitcast.244, s32[512]{0:T(512)S(1)} %iota_add_fusion.2, f32[8192]{0:T(1024)S(1)} %select_maximum_fusion.2), kind=kLoop, calls=%fused_computation.8.clone.1 | loop fusion | flops 20955136 | bytes 16910336 | tf_op jit(solution)/shard_map/while/body/eval_jaxpr/reduce_sum | solution.py:94
  335.2 9.2 %fusion.74 = (f32[8192]{0:T(1024)S(1)}, f32[512,8192]{1,0:T(8,128)}) fusion(f32[512]{0:T(512)S(1)} %bitcast.243, bf16[8192,256]{1,0:T(8,128)(2,1)} %get-tuple-element.234, bf16[2,512,256]{2,1,0:T(8,128)(2,1)S(1)} %get-tuple-element.233, s32[]{:T(128)} %get-tuple-element.216), kind=kOutput, calls=%fused_computation.130.clone.1 | convolution fusion | flops 2160058368 | bytes 21268484 | tf_op jit(solution)/shard_map/while/body/eval_jaxpr/dot_general | solution.py:86
  344.5 0.6 dynamic_slice.94
  345.7 8.1 %fusion.75 = (f32[8192]{0:T(1024)S(1)}, f32[8192]{0:T(1024)S(1)}) fusion(f32[512,8192]{1,0:T(8,128)} %get-tuple-element.198, s32[8192]{0:T(1024)S(1)} %bitcast.244, s32[512]{0:T(512)S(1)} %iota_add_fusion.2, f32[8192]{0:T(1024)S(1)} %select_maximum_fusion.2), kind=kLoop, calls=%fused_computation.8.clone.1 | loop fusion | flops 20955136 | bytes 16910336 | tf_op jit(solution)/shard_map/while/body/eval_jaxpr/reduce_sum | solution.py:94
  353.9 10.9 %all-gather.1 = f32[384,256]{1,0:T(8,128)S(1)} all-gather(f32[96,256]{1,0:T(8,128)S(1)} %pad_maximum_fusion), channel_id=3, replica_groups=mesh['dp'=2,'tensor'=4,'pool_0'=4,'pool_1'=4,'pool_2'=2] {'pool_0'}, dimensions={0}, use_global_device_ids=true | all-gather | bytes 491520 | tf_op jit(solution)/shard_map/all_gather | solution.py:31
  364.9 11.7 %all-gather.2 = f32[384,256]{1,0:T(8,128)S(1)} all-gather(f32[96,256]{1,0:T(8,128)S(1)} %pad_maximum_fusion.1), channel_id=4, replica_groups=mesh['dp'=2,'tensor'=4,'pool_0'=4,'pool_1'=4,'pool_2'=2] {'pool_1'}, dimensions={0}, use_global_device_ids=true | all-gather | bytes 491520 | tf_op jit(solution)/shard_map/all_gather | solution.py:31
  376.7 7.7 %all-gather.3 = f32[192,256]{1,0:T(8,128)S(1)} all-gather(f32[96,256]{1,0:T(8,128)S(1)} %pad_maximum_fusion.2), channel_id=5, replica_groups=mesh['dp'=2,'tensor'=4,'pool_0'=4,'pool_1'=4,'pool_2'=2] {'pool_2'}, dimensions={0}, use_global_device_ids=true | all-gather | bytes 294912 | tf_op jit(solution)/shard_map/all_gather | solution.py:31
  384.4 2.6 scatter_fusion
  387.0 0.7 fusion.54
  387.7 0.1 copy-done.1
  (75 shorter events, 1.0 us)
Async XLA Ops:
  7.2 240.4 %copy-start = (bf16[1048576]{0:T(1024)(128)(2,1)S(1)}, bf16[1048576]{0:T(1024)(128)(2,1)}, u32[]{:S(2)}) copy-start(bf16[1048576]{0:T(1024)(128)(2,1)} %param.17) | copy-start | bytes 6291460
  7.2 309.3 %all-gather.7.cloned.1.call-start = ((), (), s32[]{:S(2)}) async-start(), calls=%async_computation.5 | async-start | bytes 4325376 | tf_op jit(solution)/shard_map/all_gather | solution.py:145
  9.4 195.2 %copy-start.6 = (bf16[1024,256]{1,0:T(8,128)(2,1)S(1)}, bf16[1024,256]{1,0:T(8,128)(2,1)}, u32[]{:S(2)}) copy-start(bf16[1024,256]{1,0:T(8,128)(2,1)} %param.14) | copy-start | bytes 1572868
  204.6 37.4 %copy-start.4 = (s32[256,1]{0,1:T(1,128)S(1)}, s32[256,1]{0,1:T(1,128)}, u32[]{:S(2)}) copy-start(s32[256,1]{0,1:T(1,128)} %param.20) | copy-start | bytes 3076
  204.6 43.0 %copy-start.3 = (s32[1024]{0:T(1024)S(1)}, s32[1024]{0:T(1024)}, u32[]{:S(2)}) copy-start(s32[1024]{0:T(1024)} %param.16) | copy-start | bytes 12292
  204.6 61.0 %copy-start.5 = (s32[1,256]{1,0:T(1,128)S(1)}, s32[1,256]{1,0:T(1,128)}, u32[]{:S(2)}) copy-start(s32[1,256]{1,0:T(1,128)} %param.18) | copy-start | bytes 3076
  204.6 111.9 %copy-start.2 = (bf16[1024,256]{1,0:T(8,128)(2,1)S(1)}, bf16[1024,256]{1,0:T(8,128)(2,1)}, u32[]{:S(2)}) copy-start(bf16[1024,256]{1,0:T(8,128)(2,1)} %param.15) | copy-start | bytes 1572868
  242.7 12.6 %all-to-all-start.2 = ((s32[32,1,32]{2,1,0:T(1,128)}), s32[32,1,32]{2,1,0:T(1,128)S(1)}, u32[]{:S(2)}, u32[]{:S(2)}) async-start(s32[32,1,32]{2,1,0:T(1,128)} %broadcast_in_dim.52), calls=%async_computation.2 | async-start | bytes 32768 | tf_op jit(solution)/shard_map/all_to_all | solution.py:51
  257.8 54.7 %all-to-all-start.3 = ((s32[32,1,16]{2,1,0:T(1,128)}), s32[32,1,16]{2,1,0:T(1,128)S(1)}, u32[]{:S(2)}, u32[]{:S(2)}) async-start(s32[32,1,16]{2,1,0:T(1,128)} %bitcast.38), calls=%async_computation.3 | async-start | bytes 32768 | tf_op jit(solution)/shard_map/all_to_all | solution.py:192
  312.5 71.9 %all-to-all-start.4 = ((bf16[32,16,256]{2,1,0:T(8,128)(2,1)}), bf16[32,16,256]{2,1,0:T(8,128)(2,1)S(1)}, u32[]{:S(2)}, u32[]{:S(2)}) async-start(bf16[32,16,256]{2,1,0:T(8,128)(2,1)} %bitcast.41), calls=%async_computation.4 | async-start | bytes 524288 | tf_op jit(solution)/shard_map/all_to_all | solution.py:185
  387.0 0.8 copy-start.1
Sparse Core Ops, SparseCore 0:
  242.1 60.3 all-gather.6
